TPU v7x, 32 devices: a whole 2x2x4 slice. The times are simulated.
32 devices in a mesh: dp: 8 (over y, x, core), tensor: 4 (over z).
Axes of the slice: x: 2, y: 2, z: 4, core: 2. Of those that a mesh axis runs over, the one named last changes fastest.
Arguments:
- layer_input: bfloat16 [16, 768, 768], P('dp', 'tensor'), may hold values from -6 to 6
- word_segments: int32 [16, 256], P('dp'), may hold values from 0 to 13, never falling along the last dimension, each value on 1 to 36 neighbouring positions
- image_order: int32 [16, 14], P('dp'), may hold values from 0 to 13, each once within a row
- cross_qkv: bfloat16 [3, 768, 768], P(None, None, 'tensor'), may hold values from -0.21875 to 0.21875
- cross_out: bfloat16 [768, 768], P('tensor'), may hold values from -0.875 to 0.875
- self_qkv: bfloat16 [2, 3, 768, 768], P(None, None, None, 'tensor'), may hold values from -0.21875 to 0.21875
- self_out: bfloat16 [2, 768, 768], P(None, 'tensor'), may hold values from -0.875 to 0.875
- ffn_up: bfloat16 [2, 768, 3072], P(None, None, 'tensor'), may hold values from -0.21875 to 0.21875
- ffn_down: bfloat16 [2, 3072, 768], P(None, 'tensor'), may hold values from -0.109375 to 0.109375
- norm_gains: float32 [5, 768], replicated, may hold values from 0.5 to 1.5
- norm_biases: float32 [5, 768], replicated, may hold values from -3 to 3
- out_grad: bfloat16 [16, 768, 768], P('dp', 'tensor'), may hold values from -6 to 6
Outputs:
- layer_output: bfloat16 [16, 768, 768], P('dp', 'tensor')
- input_grad: float32 [16, 768, 768], P('dp', 'tensor')
- cross_qkv_grad: float32 [3, 768, 768], P(None, None, 'tensor')
- cross_out_grad: float32 [768, 768], P('tensor')
- self_qkv_grad: float32 [2, 3, 768, 768], P(None, None, None, 'tensor')
- self_out_grad: float32 [2, 768, 768], P(None, 'tensor')
- ffn_up_grad: float32 [2, 768, 3072], P(None, None, 'tensor')
- ffn_down_grad: float32 [2, 3072, 768], P(None, 'tensor')
- norm_gains_grad: float32 [5, 768], replicated
- norm_biases_grad: float32 [5, 768], replicated
Inputs may be any that keep to these rules, and one draw needn't show every extreme that they name: `word_segments`: in each row the ids never fall along the word slots, and each of the 14 captions has 1 to 36 slots. `image_order`: each row names every image once.
All inputs are finite; a program needn't handle non-finite values.
Results may differ from a plain program's by a relative error of at most 0.035.
Values may be sent and summed in bfloat16 or wider, within the bound.
A program may use at most 192 MiB of HBM per device.

v0:
```python
import jax
import jax.numpy as jnp
from jax import lax
from jax.sharding import PartitionSpec as P

HEAD_DIM = 64
WORDS = 256
CAPTIONS = 14
BOXES = 36
REGIONS = 504
PADS = 8
NORM_EPSILON = 1e-12


def contract_in(hidden, w_words, w_regions):
    if w_regions is None:
        return jnp.einsum("rsd,dc->rsc", hidden, w_words, preferred_element_type=jnp.float32)
    return jnp.concatenate(
        [
            jnp.einsum(
                "rsd,dc->rsc", hidden[:, :WORDS], w_words, preferred_element_type=jnp.float32
            ),
            jnp.einsum(
                "rsd,dc->rsc", hidden[:, WORDS:], w_regions, preferred_element_type=jnp.float32
            ),
        ],
        axis=1,
    )


def contract_back(grad_b, w_words, w_regions):
    if w_regions is None:
        return jnp.einsum("rsc,dc->rsd", grad_b, w_words, preferred_element_type=jnp.float32)
    return jnp.concatenate(
        [
            jnp.einsum(
                "rsc,dc->rsd", grad_b[:, :WORDS], w_words, preferred_element_type=jnp.float32
            ),
            jnp.einsum(
                "rsc,dc->rsd", grad_b[:, WORDS:], w_regions, preferred_element_type=jnp.float32
            ),
        ],
        axis=1,
    )


def weight_grad(hidden, grad_b, by_modality):
    if not by_modality:
        return jnp.einsum("rsd,rsc->dc", hidden, grad_b, preferred_element_type=jnp.float32)
    return jnp.stack(
        [
            jnp.einsum(
                "rsd,rsc->dc",
                hidden[:, :WORDS],
                grad_b[:, :WORDS],
                preferred_element_type=jnp.float32,
            ),
            jnp.einsum(
                "rsd,rsc->dc",
                hidden[:, WORDS:],
                grad_b[:, WORDS:],
                preferred_element_type=jnp.float32,
            ),
        ],
        axis=0,
    )


def head_split(tensor_b):
    return tensor_b.reshape(
        tensor_b.shape[0], tensor_b.shape[1], tensor_b.shape[2] // HEAD_DIM, HEAD_DIM
    )


def masked_scores(query_heads, key_heads, allowed):
    raw_scores = jnp.einsum(
        "rqhd,rkhd->rhqk", query_heads, key_heads, preferred_element_type=jnp.float32
    ) * HEAD_DIM ** (-0.5)
    return jnp.where(allowed[:, None], raw_scores, -1e30)


def region_matrix(table, member):
    if table is None:
        return None
    return table[member]


def attend(hidden, qkv_words, qkv_regions, out_words, out_regions, allowed):
    projected = [
        contract_in(hidden, qkv_words[member], region_matrix(qkv_regions, member)).astype(
            jnp.bfloat16
        )
        for member in range(3)
    ]
    query_b, key_b, value_b = projected
    scores = masked_scores(head_split(query_b), head_split(key_b), allowed)
    top_score = jnp.max(scores, axis=-1, keepdims=True)
    exponent = jnp.exp(scores - top_score)
    denominator = jnp.sum(exponent, axis=-1, keepdims=True)
    attention_probs = exponent / denominator
    log_total = top_score + jnp.log(denominator)
    context_b = (
        jnp.einsum(
            "rhqk,rkhd->rqhd",
            attention_probs.astype(jnp.bfloat16),
            head_split(value_b),
            preferred_element_type=jnp.float32,
        )
        .reshape(query_b.shape)
        .astype(jnp.bfloat16)
    )
    partial_out = contract_in(context_b, out_words, out_regions)
    return (partial_out, (query_b, key_b, value_b, log_total, context_b))


def attend_back(
    hidden, grad_b, kept_values, qkv_words, qkv_regions, out_words, out_regions, allowed
):
    query_b, key_b, value_b, log_total, context_b = kept_values
    by_modality = qkv_regions is not None
    out_weight_grad = weight_grad(context_b, grad_b, by_modality)
    context_grad = head_split(contract_back(grad_b, out_words, out_regions).astype(jnp.bfloat16))
    query_heads = head_split(query_b)
    key_heads = head_split(key_b)
    attention_probs = jnp.exp(masked_scores(query_heads, key_heads, allowed) - log_total)
    probs_grad = jnp.einsum(
        "rqhd,rkhd->rhqk", context_grad, head_split(value_b), preferred_element_type=jnp.float32
    )
    score_grad = (
        attention_probs
        * (probs_grad - jnp.sum(attention_probs * probs_grad, axis=-1, keepdims=True))
    ).astype(jnp.bfloat16)
    scaling = HEAD_DIM ** (-0.5)
    query_grad = (
        (
            jnp.einsum("rhqk,rkhd->rqhd", score_grad, key_heads, preferred_element_type=jnp.float32)
            * scaling
        )
        .reshape(query_b.shape)
        .astype(jnp.bfloat16)
    )
    key_grad = (
        (
            jnp.einsum(
                "rhqk,rqhd->rkhd", score_grad, query_heads, preferred_element_type=jnp.float32
            )
            * scaling
        )
        .reshape(key_b.shape)
        .astype(jnp.bfloat16)
    )
    value_grad = (
        jnp.einsum(
            "rhqk,rqhd->rkhd",
            attention_probs.astype(jnp.bfloat16),
            context_grad,
            preferred_element_type=jnp.float32,
        )
        .reshape(value_b.shape)
        .astype(jnp.bfloat16)
    )
    member_grads = [query_grad, key_grad, value_grad]
    qkv_grad = jnp.stack(
        [weight_grad(hidden, member_grads[member], by_modality) for member in range(3)],
        axis=1 if by_modality else 0,
    )
    hidden_grad = contract_back(query_grad, qkv_words[0], region_matrix(qkv_regions, 0))
    hidden_grad = hidden_grad + contract_back(key_grad, qkv_words[1], region_matrix(qkv_regions, 1))
    hidden_grad = hidden_grad + contract_back(
        value_grad, qkv_words[2], region_matrix(qkv_regions, 2)
    )
    return (hidden_grad, qkv_grad, out_weight_grad)


def norm_forward(summed, gain_rows, shift_rows):
    center = summed - jnp.mean(summed, axis=-1, keepdims=True)
    inverse = lax.rsqrt(jnp.mean(center * center, axis=-1, keepdims=True) + NORM_EPSILON)
    normed = center * inverse
    return (normed * gain_rows + shift_rows, normed, inverse)


def norm_backward(upstream, normed, inverse, gain_rows):
    scaled = upstream * gain_rows
    return inverse * (
        scaled
        - jnp.mean(scaled, axis=-1, keepdims=True)
        - normed * jnp.mean(scaled * normed, axis=-1, keepdims=True)
    )


def exact_gelu(values):
    return jax.nn.gelu(values, approximate=False)


def spread(piece_b):
    return lax.all_gather(piece_b, "tensor", axis=1, tiled=True)


def collect(partial_grad):
    return lax.psum_scatter(
        partial_grad.astype(jnp.bfloat16), "tensor", scatter_dimension=1, tiled=True
    ).astype(jnp.float32)


def widen(piece_b):
    return spread(piece_b)


def finish(partial_out):
    return lax.psum_scatter(
        partial_out.astype(jnp.bfloat16), "tensor", scatter_dimension=1, tiled=True
    ).astype(jnp.float32)


def back_sum(partial_grad):
    return collect(partial_grad)


def body(
    layer_input,
    word_segments,
    image_order,
    cross_qkv,
    cross_out,
    self_qkv,
    self_out,
    ffn_up,
    ffn_down,
    norm_gains,
    norm_biases,
    out_grad,
):
    row_count = layer_input.shape[0]
    share_len = layer_input.shape[1]
    slot_count = share_len * lax.axis_size("tensor")
    tensor_place = lax.axis_index("tensor")
    groups = jnp.concatenate(
        [
            word_segments,
            jnp.repeat(image_order, BOXES, axis=1),
            jnp.full((row_count, PADS), CAPTIONS, jnp.int32),
        ],
        axis=1,
    )
    slot_ids = jnp.arange(slot_count)
    slot_kind = jnp.where(slot_ids < WORDS, 0, jnp.where(slot_ids < WORDS + REGIONS, 1, 2))
    same_group = groups[:, :, None] == groups[:, None, :]
    differ = slot_kind[:, None] != slot_kind[None, :]
    cross_ok = same_group & (differ | (slot_kind[:, None] == 2))[None]
    self_ok = same_group & jnp.logical_not(differ)[None]
    stream_ids = tensor_place * share_len + jnp.arange(share_len)
    stream_word = (stream_ids < WORDS)[:, None]
    own_rows = (stream_ids // share_len == tensor_place).astype(jnp.float32)[:, None]
    word_weight = stream_word.astype(jnp.float32) * own_rows
    other_weight = own_rows - word_weight

    def pick(table, first_norm, second_norm):
        return jnp.where(stream_word, table[first_norm], table[second_norm])

    def norm_terms(upstream, normed, first_norm, second_norm, gain_grad, bias_grad):
        gain_terms = upstream * normed
        gain_grad = gain_grad.at[first_norm].add(jnp.sum(gain_terms * word_weight, axis=(0, 1)))
        gain_grad = gain_grad.at[second_norm].add(jnp.sum(gain_terms * other_weight, axis=(0, 1)))
        bias_grad = bias_grad.at[first_norm].add(jnp.sum(upstream * word_weight, axis=(0, 1)))
        bias_grad = bias_grad.at[second_norm].add(jnp.sum(upstream * other_weight, axis=(0, 1)))
        return (gain_grad, bias_grad)

    input_full = spread(layer_input)
    stream = layer_input.astype(jnp.float32)
    cross_part, cross_kept = attend(input_full, cross_qkv, None, cross_out, None, cross_ok)
    section_one, normed_one, inverse_one = norm_forward(
        stream + finish(cross_part), norm_gains[0], norm_biases[0]
    )
    one_full = widen(section_one.astype(jnp.bfloat16))
    self_part, self_kept = attend(
        one_full, self_qkv[0], self_qkv[1], self_out[0], self_out[1], self_ok
    )
    gains_two = pick(norm_gains, 1, 2)
    section_two, normed_two, inverse_two = norm_forward(
        section_one + finish(self_part), gains_two, pick(norm_biases, 1, 2)
    )
    two_full = widen(section_two.astype(jnp.bfloat16))
    upward = contract_in(two_full, ffn_up[0], ffn_up[1])
    active, gelu_pull = jax.vjp(exact_gelu, upward)
    active_b = active.astype(jnp.bfloat16)
    ffn_part = contract_in(active_b, ffn_down[0], ffn_down[1])
    gains_three = pick(norm_gains, 3, 4)
    result, normed_three, inverse_three = norm_forward(
        section_two + finish(ffn_part), gains_three, pick(norm_biases, 3, 4)
    )
    layer_output = result.astype(jnp.bfloat16)
    upstream = out_grad.astype(jnp.float32)
    gain_grad, bias_grad = norm_terms(
        upstream, normed_three, 3, 4, jnp.zeros_like(norm_gains), jnp.zeros_like(norm_biases)
    )
    grad_three = norm_backward(upstream, normed_three, inverse_three, gains_three)
    three_full = widen(grad_three.astype(jnp.bfloat16))
    down_grad = weight_grad(active_b, three_full, True)
    active_grad = contract_back(three_full, ffn_down[0], ffn_down[1])
    upward_grad = gelu_pull(active_grad)[0].astype(jnp.bfloat16)
    up_grad = weight_grad(two_full, upward_grad, True)
    section_two_grad = grad_three + back_sum(contract_back(upward_grad, ffn_up[0], ffn_up[1]))
    gain_grad, bias_grad = norm_terms(section_two_grad, normed_two, 1, 2, gain_grad, bias_grad)
    grad_two = norm_backward(section_two_grad, normed_two, inverse_two, gains_two)
    two_back = widen(grad_two.astype(jnp.bfloat16))
    hidden_two, self_qkv_grad, self_out_grad = attend_back(
        one_full, two_back, self_kept, self_qkv[0], self_qkv[1], self_out[0], self_out[1], self_ok
    )
    section_one_grad = grad_two + back_sum(hidden_two)
    gain_grad, bias_grad = norm_terms(section_one_grad, normed_one, 0, 0, gain_grad, bias_grad)
    grad_one = norm_backward(section_one_grad, normed_one, inverse_one, norm_gains[0])
    one_back = widen(grad_one.astype(jnp.bfloat16))
    hidden_one, cross_qkv_grad, cross_out_grad = attend_back(
        input_full, one_back, cross_kept, cross_qkv, None, cross_out, None, cross_ok
    )
    input_grad = grad_one + collect(hidden_one)
    summed_grads = [
        total.astype(jnp.float32)
        for total in lax.psum(
            [
                grad.astype(jnp.bfloat16)
                for grad in (
                    cross_qkv_grad,
                    cross_out_grad,
                    self_qkv_grad,
                    self_out_grad,
                    up_grad,
                    down_grad,
                )
            ],
            "dp",
        )
    ]
    norm_grads = lax.psum((gain_grad, bias_grad), ("dp", "tensor"))
    return (
        layer_output,
        input_grad,
        summed_grads[0],
        summed_grads[1],
        summed_grads[2],
        summed_grads[3],
        summed_grads[4],
        summed_grads[5],
        norm_grads[0],
        norm_grads[1],
    )


def solution(mesh):
    in_specs = (
        P("dp", "tensor", None),
        P("dp", None),
        P("dp", None),
        P(None, None, "tensor"),
        P("tensor", None),
        P(None, None, None, "tensor"),
        P(None, "tensor", None),
        P(None, None, "tensor"),
        P(None, "tensor", None),
        P(),
        P(),
        P("dp", "tensor", None),
    )
    out_specs = (
        P("dp", "tensor", None),
        P("dp", "tensor", None),
        P(None, None, "tensor"),
        P("tensor", None),
        P(None, None, None, "tensor"),
        P(None, "tensor", None),
        P(None, None, "tensor"),
        P(None, "tensor", None),
        P(),
        P(),
    )
    return jax.shard_map(body, mesh=mesh, in_specs=in_specs, out_specs=out_specs, check_vma=False)
```

profile of v0, /device:TPU:0, one launch (start us, length us, event | category | flops | bytes accessed | tf_op | source)
XLA Modules:
  0.0 923.2 jit_solution(17433531163479221925)
XLA Ops:
  10.3 2.4 compare_and_fusion.1
  12.7 50.1 %all-gather.7.cloned.1.call-done = bf16[2,768,768]{2,1,0:T(8,128)(2,1)} async-done(((bf16[2,192,768]{2,1,0:T(8,128)(2,1)}), bf16[2,768,768]{2,1,0:T(8,128)(2,1)}) %all-gather.7.cloned.1.call-update) | async-done | bytes 2359312 | tf_op jit(solution)/shard_map/all_gather | solution.py:196
  62.8 2.7 convolution_convert_fusion.8
  66.5 6.6 fusion.228
  73.1 6.9 fusion
  80.9 6.7 fusion.59
  88.5 2.2 convolution_convert_fusion
  91.5 46.3 %reduce-scatter.7.cloned.1.call-done = bf16[2,192,768]{2,1,0:T(8,128)(2,1)} async-done(((bf16[2,768,768]{2,1,0:T(8,128)(2,1)}), bf16[2,192,768]{2,1,0:T(8,128)(2,1)}) %reduce-scatter.7.cloned.1.call-update) | async-done | bytes 589840 | tf_op jit(solution)/shard_map/reduce_scatter | solution.py:210
  143.1 48.7 %all-gather.9.cloned.1.call-done = bf16[2,768,768]{2,1,0:T(8,128)(2,1)} async-done(((bf16[2,192,768]{2,1,0:T(8,128)(2,1)}), bf16[2,768,768]{2,1,0:T(8,128)(2,1)}) %all-gather.9.cloned.1.call-update) | async-done | bytes 2359312 | tf_op jit(solution)/shard_map/all_gather | solution.py:196
  196.8 6.5 fusion.229
  203.3 6.9 fusion.1
  211.3 6.6 fusion.58
  222.9 44.8 %reduce-scatter.9.cloned.1.call-done = bf16[2,192,768]{2,1,0:T(8,128)(2,1)} async-done(((bf16[2,768,768]{2,1,0:T(8,128)(2,1)}), bf16[2,192,768]{2,1,0:T(8,128)(2,1)}) %reduce-scatter.9.cloned.1.call-update) | async-done | bytes 589840 | tf_op jit(solution)/shard_map/reduce_scatter | solution.py:210
  271.2 49.7 %all-gather.11.cloned.1.call-done = bf16[2,768,768]{2,1,0:T(8,128)(2,1)} async-done(((bf16[2,192,768]{2,1,0:T(8,128)(2,1)}), bf16[2,768,768]{2,1,0:T(8,128)(2,1)}) %all-gather.11.cloned.1.call-update) | async-done | bytes 2359312 | tf_op jit(solution)/shard_map/all_gather | solution.py:196
  320.9 2.4 fusion.102
  323.4 3.4 fusion.46
  326.8 11.2 %multiply_convert_fusion.2 = (bf16[2,768,768]{2,1,0:T(8,128)(2,1)S(1)}, f32[2,768,768]{2,1,0:T(8,128)}) fusion(f32[2,512,768]{2,1,0:T(8,128)S(1)} %fusion.46, f32[2,256,768]{2,1,0:T(8,128)S(1)} %fusion.102), kind=kLoop, calls=%fused_computation.33 | loop fusion | flops 77856768 | bytes 11796480 | tf_op jit(solution)/shard_map/convert_element_type | solution.py:285
  342.5 46.9 %reduce-scatter.11.cloned.1.call-done = bf16[2,192,768]{2,1,0:T(8,128)(2,1)} async-done(((bf16[2,768,768]{2,1,0:T(8,128)(2,1)}), bf16[2,192,768]{2,1,0:T(8,128)(2,1)}) %reduce-scatter.11.cloned.1.call-update) | async-done | bytes 589840 | tf_op jit(solution)/shard_map/reduce_scatter | solution.py:210
  394.4 50.1 %all-gather.13.cloned.1.call-done = bf16[2,768,768]{2,1,0:T(8,128)(2,1)} async-done(((bf16[2,192,768]{2,1,0:T(8,128)(2,1)}), bf16[2,768,768]{2,1,0:T(8,128)(2,1)}) %all-gather.13.cloned.1.call-update) | async-done | bytes 2359312 | tf_op jit(solution)/shard_map/all_gather | solution.py:196
  444.5 2.5 fusion.96
  447.0 3.0 fusion.41
  450.0 3.8 add_convert_fusion.1
  457.9 46.8 %reduce-scatter.13.cloned.1.call-done = bf16[2,192,768]{2,1,0:T(8,128)(2,1)} async-done(((bf16[2,768,768]{2,1,0:T(8,128)(2,1)}), bf16[2,192,768]{2,1,0:T(8,128)(2,1)}) %reduce-scatter.13.cloned.1.call-update) | async-done | bytes 589840 | tf_op jit(solution)/shard_map/reduce_scatter | solution.py:200
  504.7 4.5 multiply_reduce_fusion.8
  513.4 48.1 %all-gather.15.cloned.1.call-done = bf16[2,768,768]{2,1,0:T(8,128)(2,1)} async-done(((bf16[2,192,768]{2,1,0:T(8,128)(2,1)}), bf16[2,768,768]{2,1,0:T(8,128)(2,1)}) %all-gather.15.cloned.1.call-update) | async-done | bytes 2359312 | tf_op jit(solution)/shard_map/all_gather | solution.py:196
  563.2 2.3 fusion.72
  565.5 7.5 fusion.52
  575.5 6.3 multiply_reduce_fusion.1
  581.8 6.9 multiply_convert_fusion.1
  588.7 2.2 fusion.49
  597.9 46.3 %reduce-scatter.15.cloned.1.call-done = bf16[2,192,768]{2,1,0:T(8,128)(2,1)} async-done(((bf16[2,768,768]{2,1,0:T(8,128)(2,1)}), bf16[2,192,768]{2,1,0:T(8,128)(2,1)}) %reduce-scatter.15.cloned.1.call-update) | async-done | bytes 589840 | tf_op jit(solution)/shard_map/reduce_scatter | solution.py:200
  644.2 3.0 multiply_reduce_fusion.6
  649.6 3.3 fusion.34
  652.9 2.2 fusion.33
  671.1 28.6 %all-gather.17.cloned.1.call-done = bf16[2,768,768]{2,1,0:T(8,128)(2,1)} async-done(((bf16[2,192,768]{2,1,0:T(8,128)(2,1)}), bf16[2,768,768]{2,1,0:T(8,128)(2,1)}) %all-gather.17.cloned.1.call-update) | async-done | bytes 2359312 | tf_op jit(solution)/shard_map/all_gather | solution.py:196
  699.7 2.6 convolution_convert_fusion.7
  702.3 7.4 fusion.55
  709.8 10.3 %multiply_reduce_fusion = (f32[2,3,768]{2,1,0:T(4,128)S(1)}, f32[2,3,768,768]{2,3,1,0:T(8,128)}) fusion(f32[2,3,768,768]{2,3,1,0:T(8,128)} %get-tuple-element.240, f32[2,3,768]{2,1,0:T(4,128)S(1)} %log_add_fusion, bf16[2,768,3,64]{1,3,2,0:T(8,128)(2,1)S(1)} %bitcast.382, bf16[2,768,3,64]{1,3,2,0:T(8,128)(2,1)S(1)} %bitcast.390), kind=kOutput, calls=%fused_computation.1 | convolution fusion | flops 463597056 | bytes 29528064 | tf_op jit(solution)/shard_map/rqhd,rkhd->rhqk/dot_general | solution.py:126
  720.1 6.9 multiply_convert_fusion
  727.1 2.2 fusion.51
  738.6 2.3 add_convert_fusion
  742.7 40.8 %all-reduce.2 = (f32[5,768]{1,0:T(8,128)}, f32[5,768]{1,0:T(8,128)}) all-reduce(f32[5,768]{1,0:T(8,128)S(1)} %scatter-add.49, f32[5,768]{1,0:T(8,128)S(1)} %scatter-add.59), channel_id=1, replica_groups=mesh['dp'=8,'tensor'=4] {'dp','tensor'}, use_global_device_ids=true, to_apply=%region_36.37 | all-reduce | flops 7680 | bytes 61440 | tf_op jit(solution)/shard_map/psum | solution.py:334
  783.5 79.2 %all-reduce.6.cloned.1.call-done = (bf16[2,3,768,192]{2,3,0,1:T(8,128)(2,1)}, bf16[3,768,192]{1,2,0:T(8,128)(2,1)}, bf16[192,768]{1,0:T(8,128)(2,1)}, bf16[2,192...) async-done(((bf16[2,3,768,192]{2,3,0,1:T(8,128)(2,1)}, bf16[3,768,192]{1,2,0:T(8,128)(2,1)}, bf16[192,768]{1,0:T(8,128)(2,1)}, ...) | async-done | bytes 8257552 | tf_op jit(solution)/shard_map/psum | solution.py:319
  864.7 2.2 convert_element_type.272
  871.3 2.5 convert_element_type.273
  874.1 2.5 convert_element_type.274
  876.7 36.9 %reduce-scatter.17.cloned.1.call-done = bf16[2,192,768]{2,1,0:T(8,128)(2,1)} async-done(((bf16[2,768,768]{2,1,0:T(8,128)(2,1)}), bf16[2,192,768]{2,1,0:T(8,128)(2,1)}) %reduce-scatter.17.cloned.1.call-update) | async-done | bytes 589840 | tf_op jit(solution)/shard_map/reduce_scatter | solution.py:200
  913.6 2.6 convert_add_fusion
  (358 shorter events, 90.1 us)
Async XLA Ops:
  7.2 81.3 %copy-start = (bf16[192,768]{1,0:T(8,128)(2,1)S(1)}, bf16[192,768]{1,0:T(8,128)(2,1)}, u32[]{:S(2)}) copy-start(bf16[192,768]{1,0:T(8,128)(2,1)} %param.40) | copy-start | bytes 884740
  7.2 55.6 %all-gather.7.cloned.1.call-start = ((), (), s32[]{:S(2)}) async-start(), calls=%async_computation.6 | async-start | bytes 2949120 | tf_op jit(solution)/shard_map/all_gather | solution.py:196
  7.9 129.9 %reduce-scatter.7.cloned.1.call-start = ((), (), s32[]{:S(2)}) async-start(), calls=%async_computation.7 | async-start | bytes 2949120 | tf_op jit(solution)/shard_map/reduce_scatter | solution.py:210
  9.6 53.2 %copy-start.38 = (bf16[3,768,192]{1,2,0:T(8,128)(2,1)S(1)}, bf16[3,768,192]{1,2,0:T(8,128)(2,1)}, u32[]{:S(2)}) copy-start(bf16[3,768,192]{1,2,0:T(8,128)(2,1)} %param.39) | copy-start | bytes 2654212
  65.6 7.5 copy-start.20
  73.1 7.9 copy-start.54
  80.0 7.7 copy-start.62
  80.9 6.8 copy-start.45
  88.5 49.3 %copy-start.1 = (bf16[2,192,768]{2,1,0:T(8,128)(2,1)S(1)}, bf16[2,192,768]{2,1,0:T(8,128)(2,1)}, u32[]{:S(2)}) copy-start(bf16[2,192,768]{2,1,0:T(8,128)(2,1)} %param.36) | copy-start | bytes 1769476
  90.8 101.1 %all-gather.9.cloned.1.call-start = ((), (), s32[]{:S(2)}) async-start(), calls=%async_computation.8 | async-start | bytes 2949120 | tf_op jit(solution)/shard_map/all_gather | solution.py:196
  91.5 50.5 %copy-start.13 = (bf16[2,3,768,192]{2,3,1,0:T(8,128)(2,1)S(1)}, bf16[2,3,768,192]{2,3,1,0:T(8,128)(2,1)}, u32[]{:S(2)}) copy-start(bf16[2,3,768,192]{2,3,1,0:T(8,128)(2,1)} %param.41) | copy-start | bytes 5308420
  141.7 126.0 %reduce-scatter.9.cloned.1.call-start = ((), (), s32[]{:S(2)}) async-start(), calls=%async_computation.9 | async-start | bytes 2949120 | tf_op jit(solution)/shard_map/reduce_scatter | solution.py:210
  143.1 52.2 %copy-start.53 = (bf16[1,1,768,192]{2,3,1,0:T(8,128)(2,1)S(1)}, bf16[1,1,768,192]{2,3,1,0:T(8,128)(2,1)}, u32[]{:S(2)}) copy-start(bf16[1,1,768,192]{2,3,1,0:T(8,128)(2,1)} %get-tuple-element.227) | copy-start | bytes 884740
  196.0 7.2 copy-start.49
  203.2 8.1 copy-start.64
  203.3 7.4 copy-start.51
  210.2 7.8 copy-start.66
  210.6 7.3 copy-start.56
  211.3 6.7 copy-start.28
  220.7 100.2 %all-gather.11.cloned.1.call-start = ((), (), s32[]{:S(2)}) async-start(), calls=%async_computation.10 | async-start | bytes 2949120 | tf_op jit(solution)/shard_map/all_gather | solution.py:196
  270.8 118.6 %reduce-scatter.11.cloned.1.call-start = ((), (), s32[]{:S(2)}) async-start(), calls=%async_computation.11 | async-start | bytes 2949120 | tf_op jit(solution)/shard_map/reduce_scatter | solution.py:210
  326.8 11.2 %copy-start.7 = (f32[2,512,768]{2,1,0:T(8,128)}, f32[2,512,768]{2,1,0:T(8,128)S(1)}, u32[]{:S(2)}) copy-start(f32[2,512,768]{2,1,0:T(8,128)S(1)} %fusion.46) | copy-start | bytes 9437188
  326.8 11.2 %copy-start.88 = (bf16[2,768,768]{2,1,0:T(8,128)(2,1)S(1)}, bf16[2,768,768]{2,1,0:T(8,128)(2,1)}, u32[]{:S(2)}) copy-start(bf16[2,768,768]{2,1,0:T(8,128)(2,1)} %param.44) | copy-start | bytes 7077892
  342.4 102.1 %all-gather.13.cloned.1.call-start = ((), (), s32[]{:S(2)}) async-start(), calls=%async_computation.12 | async-start | bytes 2949120 | tf_op jit(solution)/shard_map/all_gather | solution.py:196
  342.5 162.2 %copy-start.68 = (f32[192]{0:T(256)}, f32[192]{0:T(256)S(1)}, u32[]{:S(2)}) copy-start(f32[192]{0:T(256)S(1)} %get-tuple-element.248) | copy-start | bytes 2308
  394.4 110.3 %reduce-scatter.13.cloned.1.call-start = ((), (), s32[]{:S(2)}) async-start(), calls=%async_computation.13 | async-start | bytes 2949120 | tf_op jit(solution)/shard_map/reduce_scatter | solution.py:200
  457.7 103.9 %all-gather.15.cloned.1.call-start = ((), (), s32[]{:S(2)}) async-start(), calls=%async_computation.14 | async-start | bytes 2949120 | tf_op jit(solution)/shard_map/all_gather | solution.py:196
  510.2 64.9 %slice-start.4 = ((s8[14155776]{0:T(1024)(128)(4,1)}), s8[1572864]{0:T(1024)(128)(4,1)S(1)}, s32[]{:S(2)}) async-start(s8[14155776]{0:T(1024)(128)(4,1)} %bitcast.357), calls=%async_computation.23 | async-start | bytes 3145728
  511.4 132.8 %reduce-scatter.15.cloned.1.call-start = ((), (), s32[]{:S(2)}) async-start(), calls=%async_computation.15 | async-start | bytes 2949120 | tf_op jit(solution)/shard_map/reduce_scatter | solution.py:200
  563.2 12.0 %slice-start.5 = ((s8[14155776]{0:T(1024)(128)(4,1)}), s8[4194304]{0:T(1024)(128)(4,1)S(1)}, s32[]{:S(2)}) async-start(s8[14155776]{0:T(1024)(128)(4,1)} %bitcast.357), calls=%async_computation.24 | async-start | bytes 8388608
  565.4 7.5 copy-start.14
  565.5 9.7 %slice-start.6 = ((s8[14155776]{0:T(1024)(128)(4,1)}), s8[4194304]{0:T(1024)(128)(4,1)S(1)}, s32[]{:S(2)}) async-start(s8[14155776]{0:T(1024)(128)(4,1)} %bitcast.357), calls=%async_computation.25 | async-start | bytes 8388608
  565.5 9.7 %slice-start.7 = ((s8[14155776]{0:T(1024)(128)(4,1)}), s8[4194304]{0:T(1024)(128)(4,1)S(1)}, s32[]{:S(2)}) async-start(s8[14155776]{0:T(1024)(128)(4,1)} %bitcast.357), calls=%async_computation.26 | async-start | bytes 8388608
  581.8 6.9 copy-start.48
  581.8 6.9 copy-start.61
  597.2 47.0 %copy-start.2 = (bf16[2,192,768]{2,1,0:T(8,128)(2,1)S(1)}, bf16[2,192,768]{2,1,0:T(8,128)(2,1)}, u32[]{:S(2)}) copy-start(bf16[2,192,768]{2,1,0:T(8,128)(2,1)} %param.36) | copy-start | bytes 1769476
  597.2 47.0 %copy-start.4 = (bf16[2,192,768]{2,1,0:T(8,128)(2,1)S(1)}, bf16[2,192,768]{2,1,0:T(8,128)(2,1)}, u32[]{:S(2)}) copy-start(bf16[2,192,768]{2,1,0:T(8,128)(2,1)} %reduce-scatter.7.cloned.1.call-done) | copy-start | bytes 1769476
  597.2 47.0 %copy-start.69 = (f32[192]{0:T(256)S(1)}, f32[192]{0:T(256)}, u32[]{:S(2)}) copy-start(f32[192]{0:T(256)} %copy-done.68) | copy-start | bytes 2308
  597.2 102.5 %all-gather.17.cloned.1.call-start = ((), (), s32[]{:S(2)}) async-start(), calls=%async_computation.16 | async-start | bytes 2949120 | tf_op jit(solution)/shard_map/all_gather | solution.py:196
  649.5 213.2 %all-reduce.6.cloned.1.call-start = ((), (), s32[]{:S(2)}) async-start(), calls=%async_computation.18 | async-start | bytes 16515072 | tf_op jit(solution)/shard_map/psum | solution.py:319
  702.2 7.5 copy-start.46
  702.3 17.8 %slice-start = ((s8[14155776]{0:T(1024)(128)(4,1)}), s8[4194304]{0:T(1024)(128)(4,1)S(1)}, s32[]{:S(2)}) async-start(s8[14155776]{0:T(1024)(128)(4,1)} %bitcast.355), calls=%async_computation.19 | async-start | bytes 8388608
  702.3 17.8 %slice-start.1 = ((s8[14155776]{0:T(1024)(128)(4,1)}), s8[4194304]{0:T(1024)(128)(4,1)S(1)}, s32[]{:S(2)}) async-start(s8[14155776]{0:T(1024)(128)(4,1)} %bitcast.355), calls=%async_computation.20 | async-start | bytes 8388608
  709.7 10.3 %slice-start.2 = ((s8[14155776]{0:T(1024)(128)(4,1)}), s8[4194304]{0:T(1024)(128)(4,1)S(1)}, s32[]{:S(2)}) async-start(s8[14155776]{0:T(1024)(128)(4,1)} %bitcast.355), calls=%async_computation.21 | async-start | bytes 8388608
  709.7 10.3 %slice-start.3 = ((s8[14155776]{0:T(1024)(128)(4,1)}), s8[1572864]{0:T(1024)(128)(4,1)S(1)}, s32[]{:S(2)}) async-start(s8[14155776]{0:T(1024)(128)(4,1)} %bitcast.355), calls=%async_computation.22 | async-start | bytes 3145728
  720.1 7.0 copy-start.25
  735.8 177.8 %reduce-scatter.17.cloned.1.call-start = ((), (), s32[]{:S(2)}) async-start(), calls=%async_computation.17 | async-start | bytes 2949120 | tf_op jit(solution)/shard_map/reduce_scatter | solution.py:200
  874.1 39.5 %copy-start.10 = (f32[2,192,768]{2,1,0:T(8,128)S(1)}, f32[2,192,768]{2,1,0:T(8,128)}, u32[]{:S(2)}) copy-start(f32[2,192,768]{2,1,0:T(8,128)} %copy-done.9) | copy-start | bytes 3538948
  (72 other events, 145.3 us)
Sparse Core Ops, SparseCore 0:
  9.6 53.1 all-gather.6
  90.9 46.8 reduce-scatter.6
  141.8 49.9 all-gather.8
  220.8 46.8 reduce-scatter.8
  270.9 49.9 all-gather.10
  342.5 46.8 reduce-scatter.10
  394.5 49.9 all-gather.12
  457.8 46.8 reduce-scatter.12
  511.6 49.9 all-gather.14
  597.3 46.8 reduce-scatter.14
  649.6 49.9 all-gather.16
  735.9 126.7 all-reduce.5
  865.2 48.4 reduce-scatter.16
where the time goes:
time: 932 us; the launch traced here: 923 us
  waiting for transfers between devices  624 us (67%)
  matrix products  124 us (13%)
  other arithmetic  96.2 us (10%)
  blocking collectives  40.8 us (4%)
  local copies, waits for them, and re-layouts  20.7 us (2%)
  between operations  16 us (2%)
    all_gather x6, waiting for transfers between devices, spread(): return lax.all_gather(piece_b, 'tensor', axis=1, tiled=True)  275 us
    reduce_scatter x3, waiting for transfers between devices, finish(): lax.psum_scatter(partial_out.astype(jnp.bfloat16), 'tensor', scatter_dime...  138 us
    reduce_scatter x3, waiting for transfers between devices, collect(): lax.psum_scatter(partial_grad.astype(jnp.bfloat16), 'tensor', scatter_dim...  130 us
    psum x1, waiting for transfers between devices, body(): lax.psum([grad.astype(jnp.bfloat16) for grad in (cross_qkv_grad, cross_ou...  79.2 us
    psum x1, blocking collectives, body(): norm_grads = lax.psum((gain_grad, bias_grad), ('dp', 'tensor'))  40.8 us
  transfers between devices with their start and end apart: 13, of which 13 were waited for; matrix products, arithmetic and copies ran while one was open for 5% of the time, Pallas kernels for 0%

commit v1 on v0

--- a/solution.py
+++ b/solution.py
@@ -331,7 +331,9 @@
             "dp",
         )
     ]
-    norm_grads = lax.psum((gain_grad, bias_grad), ("dp", "tensor"))
+    norm_grads = (gain_grad, bias_grad)
+    for over in ("tensor", "dp"):
+        norm_grads = lax.psum(norm_grads, over)
     return (
         layer_output,
         input_grad,

time: 932 us -> 932 us (level)
    psum x1 -> x2, blocking collectives: 40.8 us -> 41.7 us  [body(): norm_grads = lax.psum(norm_grads, over)]
where the time goes in v1:
time: 932 us; the launch traced here: 923 us
  waiting for transfers between devices  623 us (67%)
  matrix products  124 us (13%)
  other arithmetic  96.3 us (10%)
  blocking collectives  41.7 us (4%)
  local copies, waits for them, and re-layouts  20.7 us (2%)
  between operations  16 us (2%)
    all_gather x6, waiting for transfers between devices, spread(): return lax.all_gather(piece_b, 'tensor', axis=1, tiled=True)  275 us
    reduce_scatter x3, waiting for transfers between devices, finish(): lax.psum_scatter(partial_out.astype(jnp.bfloat16), 'tensor', scatter_dime...  138 us
    reduce_scatter x3, waiting for transfers between devices, collect(): lax.psum_scatter(partial_grad.astype(jnp.bfloat16), 'tensor', scatter_dim...  130 us
    psum x1, waiting for transfers between devices, body(): lax.psum([grad.astype(jnp.bfloat16) for grad in (cross_qkv_grad, cross_ou...  78.3 us
    psum x2, blocking collectives, body(): norm_grads = lax.psum(norm_grads, over)  41.7 us
  transfers between devices with their start and end apart: 13, of which 13 were waited for; matrix products, arithmetic and copies ran while one was open for 5% of the time, Pallas kernels for 0%

profile of v1, /device:TPU:0, one launch (start us, length us, event | category | flops | bytes accessed | tf_op | source)
XLA Modules:
  0.0 923.2 jit_solution(14335918508543927066)
XLA Ops:
  10.3 2.4 compare_and_fusion.1
  12.7 50.1 %all-gather.7.cloned.1.call-done = bf16[2,768,768]{2,1,0:T(8,128)(2,1)} async-done(((bf16[2,192,768]{2,1,0:T(8,128)(2,1)}), bf16[2,768,768]{2,1,0:T(8,128)(2,1)}) %all-gather.7.cloned.1.call-update) | async-done | bytes 2359312 | tf_op jit(solution)/shard_map/all_gather | solution.py:196
  62.8 2.7 convolution_convert_fusion.8
  66.5 6.6 fusion.228
  73.1 6.9 fusion
  80.9 6.7 fusion.59
  88.5 2.2 convolution_convert_fusion
  91.5 46.3 %reduce-scatter.7.cloned.1.call-done = bf16[2,192,768]{2,1,0:T(8,128)(2,1)} async-done(((bf16[2,768,768]{2,1,0:T(8,128)(2,1)}), bf16[2,192,768]{2,1,0:T(8,128)(2,1)}) %reduce-scatter.7.cloned.1.call-update) | async-done | bytes 589840 | tf_op jit(solution)/shard_map/reduce_scatter | solution.py:210
  143.1 48.7 %all-gather.9.cloned.1.call-done = bf16[2,768,768]{2,1,0:T(8,128)(2,1)} async-done(((bf16[2,192,768]{2,1,0:T(8,128)(2,1)}), bf16[2,768,768]{2,1,0:T(8,128)(2,1)}) %all-gather.9.cloned.1.call-update) | async-done | bytes 2359312 | tf_op jit(solution)/shard_map/all_gather | solution.py:196
  196.8 6.5 fusion.229
  203.3 6.9 fusion.1
  211.3 6.6 fusion.58
  222.9 44.8 %reduce-scatter.9.cloned.1.call-done = bf16[2,192,768]{2,1,0:T(8,128)(2,1)} async-done(((bf16[2,768,768]{2,1,0:T(8,128)(2,1)}), bf16[2,192,768]{2,1,0:T(8,128)(2,1)}) %reduce-scatter.9.cloned.1.call-update) | async-done | bytes 589840 | tf_op jit(solution)/shard_map/reduce_scatter | solution.py:210
  271.2 49.7 %all-gather.11.cloned.1.call-done = bf16[2,768,768]{2,1,0:T(8,128)(2,1)} async-done(((bf16[2,192,768]{2,1,0:T(8,128)(2,1)}), bf16[2,768,768]{2,1,0:T(8,128)(2,1)}) %all-gather.11.cloned.1.call-update) | async-done | bytes 2359312 | tf_op jit(solution)/shard_map/all_gather | solution.py:196
  320.9 2.4 fusion.102
  323.4 3.4 fusion.46
  326.8 11.2 %multiply_convert_fusion.2 = (bf16[2,768,768]{2,1,0:T(8,128)(2,1)S(1)}, f32[2,768,768]{2,1,0:T(8,128)}) fusion(f32[2,512,768]{2,1,0:T(8,128)S(1)} %fusion.46, f32[2,256,768]{2,1,0:T(8,128)S(1)} %fusion.102), kind=kLoop, calls=%fused_computation.33 | loop fusion | flops 77856768 | bytes 11796480 | tf_op jit(solution)/shard_map/convert_element_type | solution.py:285
  342.5 46.9 %reduce-scatter.11.cloned.1.call-done = bf16[2,192,768]{2,1,0:T(8,128)(2,1)} async-done(((bf16[2,768,768]{2,1,0:T(8,128)(2,1)}), bf16[2,192,768]{2,1,0:T(8,128)(2,1)}) %reduce-scatter.11.cloned.1.call-update) | async-done | bytes 589840 | tf_op jit(solution)/shard_map/reduce_scatter | solution.py:210
  394.4 50.1 %all-gather.13.cloned.1.call-done = bf16[2,768,768]{2,1,0:T(8,128)(2,1)} async-done(((bf16[2,192,768]{2,1,0:T(8,128)(2,1)}), bf16[2,768,768]{2,1,0:T(8,128)(2,1)}) %all-gather.13.cloned.1.call-update) | async-done | bytes 2359312 | tf_op jit(solution)/shard_map/all_gather | solution.py:196
  444.5 2.5 fusion.96
  447.0 3.0 fusion.41
  450.0 3.8 add_convert_fusion.1
  457.9 46.8 %reduce-scatter.13.cloned.1.call-done = bf16[2,192,768]{2,1,0:T(8,128)(2,1)} async-done(((bf16[2,768,768]{2,1,0:T(8,128)(2,1)}), bf16[2,192,768]{2,1,0:T(8,128)(2,1)}) %reduce-scatter.13.cloned.1.call-update) | async-done | bytes 589840 | tf_op jit(solution)/shard_map/reduce_scatter | solution.py:200
  504.7 4.5 multiply_reduce_fusion.8
  513.4 48.1 %all-gather.15.cloned.1.call-done = bf16[2,768,768]{2,1,0:T(8,128)(2,1)} async-done(((bf16[2,192,768]{2,1,0:T(8,128)(2,1)}), bf16[2,768,768]{2,1,0:T(8,128)(2,1)}) %all-gather.15.cloned.1.call-update) | async-done | bytes 2359312 | tf_op jit(solution)/shard_map/all_gather | solution.py:196
  563.2 2.3 fusion.72
  565.5 7.5 fusion.52
  575.5 6.3 multiply_reduce_fusion.1
  581.8 6.9 multiply_convert_fusion.1
  588.8 2.2 fusion.49
  598.0 46.3 %reduce-scatter.15.cloned.1.call-done = bf16[2,192,768]{2,1,0:T(8,128)(2,1)} async-done(((bf16[2,768,768]{2,1,0:T(8,128)(2,1)}), bf16[2,192,768]{2,1,0:T(8,128)(2,1)}) %reduce-scatter.15.cloned.1.call-update) | async-done | bytes 589840 | tf_op jit(solution)/shard_map/reduce_scatter | solution.py:200
  644.2 3.0 multiply_reduce_fusion.6
  649.6 3.3 fusion.34
  652.9 2.2 fusion.33
  671.1 28.6 %all-gather.17.cloned.1.call-done = bf16[2,768,768]{2,1,0:T(8,128)(2,1)} async-done(((bf16[2,192,768]{2,1,0:T(8,128)(2,1)}), bf16[2,768,768]{2,1,0:T(8,128)(2,1)}) %all-gather.17.cloned.1.call-update) | async-done | bytes 2359312 | tf_op jit(solution)/shard_map/all_gather | solution.py:196
  699.7 2.6 convolution_convert_fusion.7
  702.3 7.4 fusion.55
  709.8 10.3 %multiply_reduce_fusion = (f32[2,3,768]{2,1,0:T(4,128)S(1)}, f32[2,3,768,768]{2,3,1,0:T(8,128)}) fusion(f32[2,3,768,768]{2,3,1,0:T(8,128)} %get-tuple-element.242, f32[2,3,768]{2,1,0:T(4,128)S(1)} %log_add_fusion, bf16[2,768,3,64]{1,3,2,0:T(8,128)(2,1)S(1)} %bitcast.382, bf16[2,768,3,64]{1,3,2,0:T(8,128)(2,1)S(1)} %bitcast.390), kind=kOutput, calls=%fused_computation.1 | convolution fusion | flops 463597056 | bytes 29528064 | tf_op jit(solution)/shard_map/rqhd,rkhd->rhqk/dot_general | solution.py:126
  720.1 6.9 multiply_convert_fusion
  727.1 2.2 fusion.51
  738.6 2.3 add_convert_fusion
  742.7 16.9 %all-reduce.3 = (f32[5,768]{1,0:T(8,128)S(1)}, f32[5,768]{1,0:T(8,128)S(1)}) all-reduce(f32[5,768]{1,0:T(8,128)S(1)} %scatter-add.49, f32[5,768]{1,0:T(8,128)S(1)} %scatter-add.59), channel_id=1, replica_groups=mesh['dp'=8,'tensor'=4] {'tensor'}, use_global_device_ids=true, to_apply=%region_36.37 | all-reduce | flops 7680 | bytes 61440 | tf_op jit(solution)/shard_map/psum | solution.py:336
  759.7 24.8 %all-reduce.2 = (f32[5,768]{1,0:T(8,128)}, f32[5,768]{1,0:T(8,128)}) all-reduce(f32[5,768]{1,0:T(8,128)S(1)} %get-tuple-element.204, f32[5,768]{1,0:T(8,128)S(1)} %get-tuple-element.205), channel_id=1, replica_groups=mesh['dp'=8,'tensor'=4] {'dp'}, use_global_device_ids=true, to_apply=%region_37.38 | all-reduce | flops 7680 | bytes 61440 | tf_op jit(solution)/shard_map/psum | solution.py:336
  784.5 78.3 %all-reduce.7.cloned.1.call-done = (bf16[2,3,768,192]{2,3,0,1:T(8,128)(2,1)}, bf16[3,768,192]{1,2,0:T(8,128)(2,1)}, bf16[192,768]{1,0:T(8,128)(2,1)}, bf16[2,192...) async-done(((bf16[2,3,768,192]{2,3,0,1:T(8,128)(2,1)}, bf16[3,768,192]{1,2,0:T(8,128)(2,1)}, bf16[192,768]{1,0:T(8,128)(2,1)}, ...) | async-done | bytes 8257552 | tf_op jit(solution)/shard_map/psum | solution.py:319
  871.3 2.5 convert_element_type.273
  874.1 2.5 convert_element_type.274
  876.7 36.9 %reduce-scatter.17.cloned.1.call-done = bf16[2,192,768]{2,1,0:T(8,128)(2,1)} async-done(((bf16[2,768,768]{2,1,0:T(8,128)(2,1)}), bf16[2,192,768]{2,1,0:T(8,128)(2,1)}) %reduce-scatter.17.cloned.1.call-update) | async-done | bytes 589840 | tf_op jit(solution)/shard_map/reduce_scatter | solution.py:200
  913.6 2.6 convert_add_fusion
  (359 shorter events, 92.2 us)
Async XLA Ops:
  7.2 81.3 %copy-start = (bf16[192,768]{1,0:T(8,128)(2,1)S(1)}, bf16[192,768]{1,0:T(8,128)(2,1)}, u32[]{:S(2)}) copy-start(bf16[192,768]{1,0:T(8,128)(2,1)} %param.40) | copy-start | bytes 884740
  7.2 55.6 %all-gather.7.cloned.1.call-start = ((), (), s32[]{:S(2)}) async-start(), calls=%async_computation.6 | async-start | bytes 2949120 | tf_op jit(solution)/shard_map/all_gather | solution.py:196
  7.9 129.9 %reduce-scatter.7.cloned.1.call-start = ((), (), s32[]{:S(2)}) async-start(), calls=%async_computation.7 | async-start | bytes 2949120 | tf_op jit(solution)/shard_map/reduce_scatter | solution.py:210
  9.6 53.2 %copy-start.38 = (bf16[3,768,192]{1,2,0:T(8,128)(2,1)S(1)}, bf16[3,768,192]{1,2,0:T(8,128)(2,1)}, u32[]{:S(2)}) copy-start(bf16[3,768,192]{1,2,0:T(8,128)(2,1)} %param.39) | copy-start | bytes 2654212
  65.6 7.5 copy-start.20
  73.1 7.9 copy-start.54
  80.0 7.7 copy-start.62
  80.9 6.8 copy-start.45
  88.5 49.3 %copy-start.1 = (bf16[2,192,768]{2,1,0:T(8,128)(2,1)S(1)}, bf16[2,192,768]{2,1,0:T(8,128)(2,1)}, u32[]{:S(2)}) copy-start(bf16[2,192,768]{2,1,0:T(8,128)(2,1)} %param.36) | copy-start | bytes 1769476
  90.8 101.1 %all-gather.9.cloned.1.call-start = ((), (), s32[]{:S(2)}) async-start(), calls=%async_computation.8 | async-start | bytes 2949120 | tf_op jit(solution)/shard_map/all_gather | solution.py:196
  91.5 50.5 %copy-start.13 = (bf16[2,3,768,192]{2,3,1,0:T(8,128)(2,1)S(1)}, bf16[2,3,768,192]{2,3,1,0:T(8,128)(2,1)}, u32[]{:S(2)}) copy-start(bf16[2,3,768,192]{2,3,1,0:T(8,128)(2,1)} %param.41) | copy-start | bytes 5308420
  141.7 126.0 %reduce-scatter.9.cloned.1.call-start = ((), (), s32[]{:S(2)}) async-start(), calls=%async_computation.9 | async-start | bytes 2949120 | tf_op jit(solution)/shard_map/reduce_scatter | solution.py:210
  143.1 52.2 %copy-start.53 = (bf16[1,1,768,192]{2,3,1,0:T(8,128)(2,1)S(1)}, bf16[1,1,768,192]{2,3,1,0:T(8,128)(2,1)}, u32[]{:S(2)}) copy-start(bf16[1,1,768,192]{2,3,1,0:T(8,128)(2,1)} %get-tuple-element.229) | copy-start | bytes 884740
  196.0 7.2 copy-start.49
  203.2 8.1 copy-start.64
  203.3 7.4 copy-start.51
  210.2 7.8 copy-start.66
  210.6 7.3 copy-start.56
  211.3 6.7 copy-start.28
  220.7 100.2 %all-gather.11.cloned.1.call-start = ((), (), s32[]{:S(2)}) async-start(), calls=%async_computation.10 | async-start | bytes 2949120 | tf_op jit(solution)/shard_map/all_gather | solution.py:196
  270.8 118.7 %reduce-scatter.11.cloned.1.call-start = ((), (), s32[]{:S(2)}) async-start(), calls=%async_computation.11 | async-start | bytes 2949120 | tf_op jit(solution)/shard_map/reduce_scatter | solution.py:210
  326.8 11.2 %copy-start.7 = (f32[2,512,768]{2,1,0:T(8,128)}, f32[2,512,768]{2,1,0:T(8,128)S(1)}, u32[]{:S(2)}) copy-start(f32[2,512,768]{2,1,0:T(8,128)S(1)} %fusion.46) | copy-start | bytes 9437188
  326.8 11.2 %copy-start.88 = (bf16[2,768,768]{2,1,0:T(8,128)(2,1)S(1)}, bf16[2,768,768]{2,1,0:T(8,128)(2,1)}, u32[]{:S(2)}) copy-start(bf16[2,768,768]{2,1,0:T(8,128)(2,1)} %param.44) | copy-start | bytes 7077892
  342.4 102.1 %all-gather.13.cloned.1.call-start = ((), (), s32[]{:S(2)}) async-start(), calls=%async_computation.12 | async-start | bytes 2949120 | tf_op jit(solution)/shard_map/all_gather | solution.py:196
  342.5 162.2 %copy-start.68 = (f32[192]{0:T(256)}, f32[192]{0:T(256)S(1)}, u32[]{:S(2)}) copy-start(f32[192]{0:T(256)S(1)} %get-tuple-element.250) | copy-start | bytes 2308
  394.4 110.3 %reduce-scatter.13.cloned.1.call-start = ((), (), s32[]{:S(2)}) async-start(), calls=%async_computation.13 | async-start | bytes 2949120 | tf_op jit(solution)/shard_map/reduce_scatter | solution.py:200
  457.7 103.9 %all-gather.15.cloned.1.call-start = ((), (), s32[]{:S(2)}) async-start(), calls=%async_computation.14 | async-start | bytes 2949120 | tf_op jit(solution)/shard_map/all_gather | solution.py:196
  510.2 64.9 %slice-start.4 = ((s8[14155776]{0:T(1024)(128)(4,1)}), s8[1572864]{0:T(1024)(128)(4,1)S(1)}, s32[]{:S(2)}) async-start(s8[14155776]{0:T(1024)(128)(4,1)} %bitcast.357), calls=%async_computation.23 | async-start | bytes 3145728
  511.4 132.8 %reduce-scatter.15.cloned.1.call-start = ((), (), s32[]{:S(2)}) async-start(), calls=%async_computation.15 | async-start | bytes 2949120 | tf_op jit(solution)/shard_map/reduce_scatter | solution.py:200
  563.2 12.0 %slice-start.5 = ((s8[14155776]{0:T(1024)(128)(4,1)}), s8[4194304]{0:T(1024)(128)(4,1)S(1)}, s32[]{:S(2)}) async-start(s8[14155776]{0:T(1024)(128)(4,1)} %bitcast.357), calls=%async_computation.24 | async-start | bytes 8388608
  565.5 7.5 copy-start.14
  565.5 9.7 %slice-start.6 = ((s8[14155776]{0:T(1024)(128)(4,1)}), s8[4194304]{0:T(1024)(128)(4,1)S(1)}, s32[]{:S(2)}) async-start(s8[14155776]{0:T(1024)(128)(4,1)} %bitcast.357), calls=%async_computation.25 | async-start | bytes 8388608
  565.5 9.7 %slice-start.7 = ((s8[14155776]{0:T(1024)(128)(4,1)}), s8[4194304]{0:T(1024)(128)(4,1)S(1)}, s32[]{:S(2)}) async-start(s8[14155776]{0:T(1024)(128)(4,1)} %bitcast.357), calls=%async_computation.26 | async-start | bytes 8388608
  581.8 6.9 copy-start.48
  581.8 6.9 copy-start.61
  597.2 47.0 %copy-start.2 = (bf16[2,192,768]{2,1,0:T(8,128)(2,1)S(1)}, bf16[2,192,768]{2,1,0:T(8,128)(2,1)}, u32[]{:S(2)}) copy-start(bf16[2,192,768]{2,1,0:T(8,128)(2,1)} %param.36) | copy-start | bytes 1769476
  597.2 47.0 %copy-start.4 = (bf16[2,192,768]{2,1,0:T(8,128)(2,1)S(1)}, bf16[2,192,768]{2,1,0:T(8,128)(2,1)}, u32[]{:S(2)}) copy-start(bf16[2,192,768]{2,1,0:T(8,128)(2,1)} %reduce-scatter.7.cloned.1.call-done) | copy-start | bytes 1769476
  597.2 47.0 %copy-start.69 = (f32[192]{0:T(256)S(1)}, f32[192]{0:T(256)}, u32[]{:S(2)}) copy-start(f32[192]{0:T(256)} %copy-done.68) | copy-start | bytes 2308
  597.2 102.5 %all-gather.17.cloned.1.call-start = ((), (), s32[]{:S(2)}) async-start(), calls=%async_computation.16 | async-start | bytes 2949120 | tf_op jit(solution)/shard_map/all_gather | solution.py:196
  649.5 213.2 %all-reduce.7.cloned.1.call-start = ((), (), s32[]{:S(2)}) async-start(), calls=%async_computation.18 | async-start | bytes 16515072 | tf_op jit(solution)/shard_map/psum | solution.py:319
  702.3 7.5 copy-start.46
  702.3 17.8 %slice-start = ((s8[14155776]{0:T(1024)(128)(4,1)}), s8[4194304]{0:T(1024)(128)(4,1)S(1)}, s32[]{:S(2)}) async-start(s8[14155776]{0:T(1024)(128)(4,1)} %bitcast.355), calls=%async_computation.19 | async-start | bytes 8388608
  702.3 17.8 %slice-start.1 = ((s8[14155776]{0:T(1024)(128)(4,1)}), s8[4194304]{0:T(1024)(128)(4,1)S(1)}, s32[]{:S(2)}) async-start(s8[14155776]{0:T(1024)(128)(4,1)} %bitcast.355), calls=%async_computation.20 | async-start | bytes 8388608
  709.8 10.3 %slice-start.2 = ((s8[14155776]{0:T(1024)(128)(4,1)}), s8[4194304]{0:T(1024)(128)(4,1)S(1)}, s32[]{:S(2)}) async-start(s8[14155776]{0:T(1024)(128)(4,1)} %bitcast.355), calls=%async_computation.21 | async-start | bytes 8388608
  709.8 10.3 %slice-start.3 = ((s8[14155776]{0:T(1024)(128)(4,1)}), s8[1572864]{0:T(1024)(128)(4,1)S(1)}, s32[]{:S(2)}) async-start(s8[14155776]{0:T(1024)(128)(4,1)} %bitcast.355), calls=%async_computation.22 | async-start | bytes 3145728
  720.1 7.0 copy-start.25
  735.8 177.8 %reduce-scatter.17.cloned.1.call-start = ((), (), s32[]{:S(2)}) async-start(), calls=%async_computation.17 | async-start | bytes 2949120 | tf_op jit(solution)/shard_map/reduce_scatter | solution.py:200
  874.1 39.5 %copy-start.10 = (f32[2,192,768]{2,1,0:T(8,128)S(1)}, f32[2,192,768]{2,1,0:T(8,128)}, u32[]{:S(2)}) copy-start(f32[2,192,768]{2,1,0:T(8,128)} %copy-done.9) | copy-start | bytes 3538948
  (72 other events, 145.5 us)
Sparse Core Ops, SparseCore 0:
  9.6 53.1 all-gather.6
  90.9 46.8 reduce-scatter.6
  141.8 49.9 all-gather.8
  220.8 46.8 reduce-scatter.8
  270.9 49.9 all-gather.10
  342.5 46.8 reduce-scatter.10
  394.5 49.9 all-gather.12
  457.8 46.8 reduce-scatter.12
  511.6 49.9 all-gather.14
  597.3 46.8 reduce-scatter.14
  649.7 49.9 all-gather.16
  735.9 126.7 all-reduce.6
  865.1 48.4 reduce-scatter.16
